TPU v7x, 32 devices: a whole 2x2x4 slice. The times are simulated.
32 devices in a mesh: dp: 8 (over z, y), head: 4 (over x, core).
Axes of the slice: x: 2, y: 2, z: 4, core: 2. Of those that a mesh axis runs over, the one named last changes fastest.
Arguments:
- tokens: bfloat16 [32768, 768], P(('dp', 'head')), may hold values from -6 to 6
- seq_lengths: int32 [8], P('dp'), may hold values from 128 to 4096, as said below
- seg_bounds: int32 [8, 65], P('dp'), may hold values from 0 to 4096, as said below
- w_qkv: bfloat16 [768, 2304], replicated, may hold values from -0.625 to 0.625
- b_qv: float32 [1536], replicated, may hold values from -6 to 6
- conv_w: float32 [12, 33], P('head'), may hold values from -0.3 to 0.3
- w_out: bfloat16 [768, 768], replicated, may hold values from -0.4375 to 0.4375
- b_out: float32 [768], replicated, may hold values from -3 to 3
- ln1_gain: float32 [768], replicated, may hold values from 0.5 to 1.5
- ln1_bias: float32 [768], replicated, may hold values from -3 to 3
- w_up: bfloat16 [768, 3072], replicated, may hold values from -0.21875 to 0.21875
- b_up: float32 [3072], replicated, may hold values from -3 to 3
- w_down: bfloat16 [3072, 768], replicated, may hold values from -0.109375 to 0.109375
- b_down: float32 [768], replicated, may hold values from -3 to 3
- ln2_gain: float32 [768], replicated, may hold values from 0.5 to 1.5
- ln2_bias: float32 [768], replicated, may hold values from -3 to 3
- cotangent: bfloat16 [32768, 768], P(('dp', 'head')), may hold values from -6 to 6
Outputs:
- out: bfloat16 [32768, 768], P(('dp', 'head'))
- grad_tokens: float32 [32768, 768], P(('dp', 'head'))
- grad_w_qkv: float32 [768, 2304], replicated
- grad_b_qv: float32 [1536], replicated
- grad_conv_w: float32 [12, 33], P('head')
- grad_w_out: float32 [768, 768], replicated
- grad_b_out: float32 [768], replicated
- grad_ln1_gain: float32 [768], replicated
- grad_ln1_bias: float32 [768], replicated
- grad_w_up: float32 [768, 3072], replicated
- grad_b_up: float32 [3072], replicated
- grad_w_down: float32 [3072, 768], replicated
- grad_b_down: float32 [768], replicated
- grad_ln2_gain: float32 [768], replicated
- grad_ln2_bias: float32 [768], replicated
- pinv_residual: float32 [8, 12], P('dp', 'head')
Inputs may be any that keep to these rules, and one draw needn't show every extreme that they name: Sequence s holds seq_lengths[s] real tokens at the start of its 4096 positions; the rest is padding. `seg_bounds`: row s rises strictly from 0 to seq_lengths[s]; every landmark segment holds one or more positions.
All inputs are finite; a program needn't handle non-finite values.
Results may differ from a plain program's by a relative error of at most 0.014.
The roundings to bfloat16 on the way count: a program that leaves them out, or rounds other values in their place, can miss the bound.
Values may be sent and summed in bfloat16 or wider, within the bound.
No kernel may reach another device: no remote copies, remote signals or barrier semaphores. Data moves between devices by JAX's collectives and lax.ppermute only.
A program may use at most 320 MiB of HBM per device.

v0:
```python
import jax
import jax.numpy as jnp
from jax import lax
from jax.sharding import PartitionSpec as P

ITERS = 6


def layer_norm(inputs, gains, offsets):
    centre = jnp.mean(inputs, axis=-1, keepdims=True)
    centred = inputs - centre
    spread = jnp.mean(centred * centred, axis=-1, keepdims=True)
    return centred * lax.rsqrt(spread + 1e-05) * gains + offsets


def gelu_exact(inputs):
    return 0.5 * inputs * (1.0 + jax.scipy.special.erf(inputs * 0.7071067811865476))


def pseudo_inverse(kernel):
    highest_precision_flag = lax.Precision.HIGHEST
    landmarks = kernel.shape[-1]
    identity = jnp.eye(landmarks, dtype=kernel.dtype)
    squares = jnp.sum(kernel * kernel, axis=(1, 2))
    inverse_approximation = jnp.swapaxes(kernel, 1, 2) / squares[:, None, None]
    for _ in range(ITERS):
        product = jnp.matmul(kernel, inverse_approximation, precision=highest_precision_flag)
        inner = 7.0 * identity - product
        inner = 15.0 * identity - jnp.matmul(product, inner, precision=highest_precision_flag)
        inner = 13.0 * identity - jnp.matmul(product, inner, precision=highest_precision_flag)
        inverse_approximation = 0.25 * jnp.matmul(
            inverse_approximation, inner, precision=highest_precision_flag
        )
    leftover = identity - jnp.matmul(
        kernel, inverse_approximation, precision=highest_precision_flag
    )
    residual = jnp.sqrt(jnp.sum(leftover * leftover, axis=(1, 2)) / landmarks)
    return (inverse_approximation, residual)


def nystrom(query_matrix, key_matrix, values, length, bounds, taps):
    highest_precision_flag = lax.Precision.HIGHEST
    positions = query_matrix.shape[0]
    scale_factor_term = query_matrix.shape[-1] ** (-0.5)
    position = jnp.arange(positions, dtype=jnp.int32)
    valid = (position < length).astype(jnp.float32)
    member_flags = (
        (position[None, :] >= bounds[:-1, None]) & (position[None, :] < bounds[1:, None])
    ).astype(jnp.float32)
    valid_count_vector = jnp.sum(member_flags, axis=1)
    query_landmark_rows = (
        jnp.einsum("ut,tvr->uvr", member_flags, query_matrix, precision=highest_precision_flag)
        / valid_count_vector[:, None, None]
    )
    key_landmark_rows = (
        jnp.einsum("ut,tvr->uvr", member_flags, key_matrix, precision=highest_precision_flag)
        / valid_count_vector[:, None, None]
    )
    first_kernel_matrix = jax.nn.softmax(
        jnp.einsum(
            "gbw,ubw->bgu", query_matrix, key_landmark_rows, precision=highest_precision_flag
        )
        * scale_factor_term,
        axis=-1,
    )
    middle_kernel_matrix = jax.nn.softmax(
        jnp.einsum(
            "ouq,puq->uop", query_landmark_rows, key_landmark_rows, precision=highest_precision_flag
        )
        * scale_factor_term,
        axis=-1,
    )
    score_matrix = (
        jnp.einsum(
            "yib,wib->iyw", query_landmark_rows, key_matrix, precision=highest_precision_flag
        )
        * scale_factor_term
    )
    score_matrix = jnp.where(valid[None, None, :] > 0.0, score_matrix, -1000000000.0)
    last_kernel_matrix = jax.nn.softmax(score_matrix, axis=-1)
    inverse_approximation, residual = pseudo_inverse(middle_kernel_matrix)
    masked_scores_matrix = values * valid[:, None, None]
    landmark_summary = jnp.einsum(
        "qbl,lqs->qbs", last_kernel_matrix, masked_scores_matrix, precision=highest_precision_flag
    )
    mixed_value_rows = jnp.einsum(
        "gki,gia->gka", inverse_approximation, landmark_summary, precision=highest_precision_flag
    )
    attended = jnp.einsum(
        "hnl,hld->nhd", first_kernel_matrix, mixed_value_rows, precision=highest_precision_flag
    )
    margin = taps.shape[1] // 2
    padded = jnp.pad(masked_scores_matrix, ((margin, margin), (0, 0), (0, 0)))
    convolved = jnp.zeros_like(masked_scores_matrix)
    for tap_index in range(taps.shape[1]):
        convolved = (
            convolved + taps[None, :, tap_index, None] * padded[tap_index : tap_index + positions]
        )
    return ((attended + convolved) * valid[:, None, None], residual)


def attend_group(joined, taps, lengths, bounds):
    group_rows = joined.shape[0]
    local_width = joined.shape[2]
    heads_local = taps.shape[0]
    seq_count = lengths.shape[0]
    shaped = joined.reshape(
        seq_count, group_rows // seq_count, 3, heads_local, local_width // heads_local
    )
    context, residual = jax.vmap(nystrom, in_axes=(0, 0, 0, 0, 0, None))(
        shaped[:, :, 0], shaped[:, :, 1], shaped[:, :, 2], lengths, bounds, taps
    )
    return (context.reshape(group_rows, local_width), residual)


def body(
    tokens,
    seq_lengths,
    seg_bounds,
    w_qkv,
    b_qv,
    conv_w,
    w_out,
    b_out,
    ln1_gain,
    ln1_bias,
    w_up,
    b_up,
    w_down,
    b_down,
    ln2_gain,
    ln2_bias,
    cotangent,
):
    tok_rows, width = tokens.shape
    group_size = lax.axis_size("head")
    seqs_local = seq_lengths.shape[0]
    bucket = tok_rows * group_size // seqs_local
    hidden_width = w_up.shape[1]
    position = lax.axis_index("head") * tok_rows + jnp.arange(tok_rows, dtype=jnp.int32)
    owner = (position // bucket)[:, None] == jnp.arange(seqs_local, dtype=jnp.int32)[None, :]
    limit = jnp.sum(jnp.where(owner, seq_lengths[None, :], 0), axis=1)
    valid = (position % bucket < limit).astype(jnp.float32)
    qkv_bias = jnp.concatenate([b_qv[:width], jnp.zeros((width,), jnp.float32), b_qv[width:]])
    projected = jnp.dot(tokens, w_qkv, preferred_element_type=jnp.float32) + qkv_bias
    projected = projected.astype(jnp.bfloat16).reshape(tok_rows, 3, width)
    by_heads = lax.all_to_all(projected, "head", split_axis=2, concat_axis=0, tiled=True)

    def attend_local(joined, taps):
        return attend_group(joined, taps, seq_lengths, seg_bounds)

    context, attend_back, residual = jax.vjp(
        attend_local, by_heads.astype(jnp.float32), conv_w, has_aux=True
    )
    context_tok = lax.all_to_all(
        context.astype(jnp.bfloat16), "head", split_axis=0, concat_axis=1, tiled=True
    )
    attn_out = jnp.dot(context_tok, w_out, preferred_element_type=jnp.float32) + b_out
    normed, norm1_back = jax.vjp(
        layer_norm, tokens.astype(jnp.float32) + attn_out, ln1_gain, ln1_bias
    )
    normed_low = normed.astype(jnp.bfloat16)
    upper = jnp.dot(normed_low, w_up, preferred_element_type=jnp.float32) + b_up
    activated, gelu_back = jax.vjp(gelu_exact, upper)
    act_low = activated.astype(jnp.bfloat16)
    ffn_out = jnp.dot(act_low, w_down, preferred_element_type=jnp.float32) + b_down
    final, norm2_back = jax.vjp(layer_norm, normed + ffn_out, ln2_gain, ln2_bias)
    result = (final * valid[:, None]).astype(jnp.bfloat16)
    d_final = cotangent.astype(jnp.float32) * valid[:, None]
    d_sum, d_gain_two, d_bias_two = norm2_back(d_final)
    d_ffn = d_sum.astype(jnp.bfloat16)
    g_down = jnp.einsum("tk,td->kd", act_low, d_ffn, preferred_element_type=jnp.float32)
    gb_down = jnp.sum(d_ffn.astype(jnp.float32), axis=0)
    d_act = jnp.einsum("td,kd->tk", d_ffn, w_down, preferred_element_type=jnp.float32)
    (d_upper,) = gelu_back(d_act)
    d_upper_low = d_upper.astype(jnp.bfloat16)
    g_up = jnp.einsum("td,tk->dk", normed_low, d_upper_low, preferred_element_type=jnp.float32)
    gb_up = jnp.sum(d_upper_low.astype(jnp.float32), axis=0)
    d_normed = d_sum + jnp.einsum(
        "tk,dk->td", d_upper_low, w_up, preferred_element_type=jnp.float32
    )
    d_resid, d_gain_one, d_bias_one = norm1_back(d_normed)
    d_attn = d_resid.astype(jnp.bfloat16)
    g_out = jnp.einsum("td,te->de", context_tok, d_attn, preferred_element_type=jnp.float32)
    gb_out = jnp.sum(d_attn.astype(jnp.float32), axis=0)
    d_context = jnp.einsum("te,de->td", d_attn, w_out, preferred_element_type=jnp.float32).astype(
        jnp.bfloat16
    )
    d_heads = lax.all_to_all(d_context, "head", split_axis=1, concat_axis=0, tiled=True)
    d_joined, d_taps = attend_back(d_heads.astype(jnp.float32))
    d_proj = lax.all_to_all(
        d_joined.astype(jnp.bfloat16), "head", split_axis=0, concat_axis=2, tiled=True
    ).reshape(tok_rows, 3 * width)
    g_qkv = jnp.einsum("td,tk->dk", tokens, d_proj, preferred_element_type=jnp.float32)
    proj_sums = jnp.sum(d_proj.astype(jnp.float32), axis=0)
    gb_qv = jnp.concatenate([proj_sums[:width], proj_sums[2 * width :]])
    d_tokens = d_resid + jnp.einsum("tk,dk->td", d_proj, w_qkv, preferred_element_type=jnp.float32)
    g_taps = lax.psum(d_taps, "dp")
    small_grads = jnp.concatenate(
        [gb_qv, gb_out, d_gain_one, d_bias_one, gb_up, gb_down, d_gain_two, d_bias_two]
    )
    flat_qkv = g_qkv.reshape(-1)
    flat_out = g_out.reshape(-1)
    flat_up = g_up.reshape(-1)
    flat_down = g_down.reshape(-1)
    part_qkv, part_out, part_up, part_down, part_small = (
        lax.psum_scatter(flat_qkv, ("dp", "head"), scatter_dimension=0, tiled=True),
        lax.psum_scatter(flat_out, ("dp", "head"), scatter_dimension=0, tiled=True),
        lax.psum_scatter(flat_up, ("dp", "head"), scatter_dimension=0, tiled=True),
        lax.psum_scatter(flat_down, ("dp", "head"), scatter_dimension=0, tiled=True),
        lax.psum_scatter(small_grads, ("dp", "head"), scatter_dimension=0, tiled=True),
    )
    full_qkv, full_out, full_up, full_down, full_small = (
        lax.all_gather(part_qkv.astype(jnp.bfloat16), ("dp", "head"), axis=0, tiled=True).astype(
            part_qkv.dtype
        ),
        lax.all_gather(part_out.astype(jnp.bfloat16), ("dp", "head"), axis=0, tiled=True).astype(
            part_out.dtype
        ),
        lax.all_gather(part_up.astype(jnp.bfloat16), ("dp", "head"), axis=0, tiled=True).astype(
            part_up.dtype
        ),
        lax.all_gather(part_down.astype(jnp.bfloat16), ("dp", "head"), axis=0, tiled=True).astype(
            part_down.dtype
        ),
        lax.all_gather(part_small.astype(jnp.bfloat16), ("dp", "head"), axis=0, tiled=True).astype(
            part_small.dtype
        ),
    )
    edges = [
        0,
        2 * width,
        3 * width,
        4 * width,
        5 * width,
        5 * width + hidden_width,
        6 * width + hidden_width,
        7 * width + hidden_width,
        8 * width + hidden_width,
    ]
    pieces = [full_small[edges[index] : edges[index + 1]] for index in range(8)]
    return (
        result,
        d_tokens,
        full_qkv.reshape(width, 3 * width),
        pieces[0],
        g_taps,
        full_out.reshape(width, width),
        pieces[1],
        pieces[2],
        pieces[3],
        full_up.reshape(width, hidden_width),
        pieces[4],
        full_down.reshape(hidden_width, width),
        pieces[5],
        pieces[6],
        pieces[7],
        residual,
    )


def solution(mesh):
    return jax.shard_map(
        body,
        mesh=mesh,
        in_specs=(
            P(("dp", "head"), None),
            P("dp"),
            P("dp", None),
            P(),
            P(),
            P("head", None),
            P(),
            P(),
            P(),
            P(),
            P(),
            P(),
            P(),
            P(),
            P(),
            P(),
            P(("dp", "head"), None),
        ),
        out_specs=(
            P(("dp", "head"), None),
            P(("dp", "head"), None),
            P(),
            P(),
            P("head", None),
            P(),
            P(),
            P(),
            P(),
            P(),
            P(),
            P(),
            P(),
            P(),
            P(),
            P("dp", "head"),
        ),
        check_vma=False,
    )
```

profile of v0, /device:TPU:0, one launch (start us, length us, event | category | flops | bytes accessed | tf_op | source)
XLA Modules:
  0.0 1377.3 jit_solution(16289387789809279403)
XLA Ops:
  9.2 7.3 add_convert_fusion.2
  16.5 6.6 copy.376
  23.1 9.1 copy.377
  32.2 5.7 all-to-all-start
  42.8 66.4 %all-to-all-done = bf16[1024,3,768]{0,1,2:T(4,128)(2,1)} async-done(((bf16[1024,3,768]{0,1,2:T(4,128)(2,1)}), bf16[1024,3,768]{0,1,2:T(4,128)(2,1)}, u32[]{:S(2)}, u32[]{:S(2)}) %all-to-all-start) | async-done | bytes 4718624 | tf_op jit(solution)/shard_map/all_to_all | solution.py:147
  113.9 5.8 copy.379
  119.7 9.2 reshape.1840
  152.9 29.3 %fusion.10 = bf16[1,4096,3,64]{1,3,2,0:T(8,128)(2,1)} fusion(f32[3,64,64]{2,1,0:T(8,128)S(1)} %copy-done.74, f32[3]{0:T(128)} %get-tuple-element.183, f32[3]{0:T(128)} %get-tuple-element.184, f32[3]{0:T(128)} %get-tuple-element.153, f32[3]{0:T(128)} %get-tuple-element.154, f32[3]{0:T(128)} %get-tuple-element.155, f32[3]{0:T(128)} %get-tuple-element.156, ...), kind=kOutput, calls=%fused_computation.26 | convolution fusion | flops 660602880 | bytes 9601420 | tf_op jit(solution)/shard_map/jvp(vmap(hnl,hld->nhd))/dot_general | solution.py:89
  200.7 13.1 all-to-all-done.1
  218.7 11.3 multiply_convert_fusion
  230.1 7.8 fusion.205
  245.6 15.1 %convert_reduce_fusion = (f32[3072]{0:T(1024)}, bf16[1024,3072]{1,0:T(8,128)(2,1)}) fusion(bf16[1024,768]{0,1:T(8,128)(2,1)S(1)} %get-tuple-element.191, bf16[3072,768]{1,0:T(8,128)(2,1)S(1)} %bitcast.688, f32[1024,3072]{1,0:T(8,128)} %get-tuple-element.253, f32[3072]{0:T(1024)S(1)} %copy-done.146), kind=kOutput, calls=%fused_computation | convolution fusion | flops 4882166784 | bytes 25190400 | tf_op jit(solution)/shard_map/td,kd->tk/dot_general | solution.py:174
  260.8 9.5 multiply_reduce_fusion.33
  284.1 16.2 %all-to-all-done.2 = bf16[1024,4,192]{0,2,1:T(8,128)(2,1)} async-done(((bf16[1024,4,192]{0,2,1:T(8,128)(2,1)}), bf16[1024,4,192]{0,2,1:T(8,128)(2,1)}, u32[]{:S(2)}, u32[]{:S(2)}) %all-to-all-start.2) | async-done | bytes 1572896 | tf_op jit(solution)/shard_map/all_to_all | solution.py:189
  305.8 5.4 reshape.1884
  311.3 6.5 fusion.13
  336.8 14.9 %multiply_reduce_fusion.30 = (f32[3]{0:T(128)}, f32[3]{0:T(128)}, f32[3]{0:T(128)}, f32[3]{0:T(128)}, f32[3]{0:T(128)}, /*index=5*/f32[3]{0:T(128)}, f32[3]{0:T(...) fusion(f32[1,4096,3,64]{1,3,2,0:T(8,128)S(1)} %copy-done.6, ...), kind=kLoop, calls=%fused_computation.77 | loop fusion | flops 25952208 | bytes 12599500 | tf_op jit(solution)/shard_map/transpose(jvp(vmap()))/reduce_sum | solution.py:97
  351.8 14.5 %broadcast_multiply_fusion.1 = (f32[1,4096,3,64]{1,3,2,0:T(8,128)}, f32[1,4096,3,64]{1,3,2,0:T(8,128)}, f32[1,4096,3,64]{1,3,2,0:T(8,128)}, f32[1,4096,3,64]{1,3...) fusion(f32[3]{0:T(128)S(1)} %copy-done.109, ...), kind=kLoop, calls=%fused_computation.117 | loop fusion | flops 11796480 | bytes 47202472 | tf_op jit(solution)/shard_map/transpose(jvp(vmap()))/mul | solution.py:97
  366.2 19.0 %broadcast_multiply_fusion = (f32[1,4096,3,64]{1,3,2,0:T(8,128)}, f32[1,4096,3,64]{1,3,2,0:T(8,128)}, f32[1,4096,3,64]{1,3,2,0:T(8,128)}, f32[1,4096,3,64]{1,3,2...) fusion(f32[3]{0:T(128)} %get-tuple-element.183, ...), kind=kLoop, calls=%fused_computation.116 | loop fusion | flops 14155776 | bytes 56639692 | tf_op jit(solution)/shard_map/transpose(jvp(vmap()))/mul | solution.py:97
  385.3 6.8 multiply_reduce_fusion.34
  404.1 5.7 fusion.7
  411.3 5.6 fusion.9
  416.8 35.5 %pad_add_fusion = f32[1,4128,3,64]{1,3,2,0:T(8,128)} fusion(f32[1,4096,3,64]{1,3,2,0:T(8,128)} %get-tuple-element.202, f32[1,4096,3,64]{1,3,2,0:T(8,128)} %get-tuple-element.203, f32[1,4096,3,64]{1,3,2,0:T(8,128)} %get-tuple-element.204, f32[1,4096,3,64]{1,3,2,0:T(8,128)} %get-tuple-element.205, f32[1,4096,3,64]{1,3,2,0:T(8,128)} %get-tuple-element.206, ...), kind=kLoop, calls=%fused_computation.30 | loop fusion | flops 20606976 | bytes 88104960 | tf_op jit(solution)/shard_map/transpose(jvp(vmap()))/add_any | solution.py:97
  452.4 15.8 %fusion.5 = f32[1,4096,1,3,64]{1,4,3,2,0:T(8,128)S(1)} fusion(f32[3,64,64]{2,1,0:T(8,128)} %fusion.207, f32[1,4096,3,64]{1,3,2,0:T(8,128)} %get-tuple-element.197, f32[1,4096,3,64]{1,3,2,0:T(8,128)} %get-tuple-element.196, f32[1,4096,3,64]{1,3,2,0:T(8,128)} %get-tuple-element.228, f32[1,4096,3,64]{1,3,2,0:T(8,128)} %get-tuple-element.199, ...), kind=kOutput, calls=%fused_computation.21 | convolution fusion | flops 611844096 | bytes 28378624 | tf_op jit(solution)/shard_map/transpose(jvp(vmap(qbl,lqs->qbs)))/dot_general | solution.py:83
  470.7 12.8 copy.437
  483.5 5.6 all-to-all-start.3
  489.2 8.5 convolution_bitcast_fusion.7
  497.7 5.9 copy.507
  511.1 9.9 fusion.216
  521.0 10.8 reshape.1881
  531.8 50.4 %all-to-all-done.3 = bf16[4096,3,192]{2,1,0:T(4,128)(2,1)} async-done(((bf16[4096,3,192]{2,1,0:T(4,128)(2,1)}), bf16[4096,3,192]{2,1,0:T(4,128)(2,1)}, u32[]{:S(2)}, u32[]{:S(2)}) %all-to-all-start.3) | async-done | bytes 4718624 | tf_op jit(solution)/shard_map/all_to_all | solution.py:191
  582.2 13.6 copy.505
  618.3 12.9 copy.439
  631.2 9.6 convolution_bitcast_fusion
  640.9 8.0 copy.441
  648.9 7.9 reshape.1872
  656.8 458.7 %all-reduce.78 = (bf16[9216]{0:T(1024)(128)(2,1)}, bf16[1769472]{0:T(1024)(128)(2,1)}, bf16[589824]{0:T(1024)(128)(2,1)}, bf16[2359296]{0:T(1024)(128)(2,1)}, bf16[2359296]{0:T(1024)(128)(2,1)}) all-reduce(f32[9216]{0:T(1024)} %constant_dynamic-update-slice_fusion, ...), channel_id=3, replica_groups=mesh['dp'=8,'head'=4] {'dp','head'}, use_global_device_ids=true, to_apply=%region_29.30.clone | all-reduce | flops 7087104 | bytes 42522624
  1126.5 5.6 squeeze.8
  1136.6 4.9 fusion.16
  1144.3 34.8 %multiply_reduce_fusion.31 = (f32[3]{0:T(128)S(1)}, f32[3]{0:T(128)S(1)}, f32[3]{0:T(128)S(1)}, f32[3]{0:T(128)S(1)}, f32[3]{0:T(128)S(1)}, /*index=5*/f32[3]{0:...) fusion(f32[1,4096,3,64]{1,3,2,0:T(8,128)} %copy-done.5, ...), kind=kLoop, calls=%fused_computation.78 | loop fusion | flops 27525064 | bytes 6308044 | tf_op jit(solution)/shard_map/transpose(jvp(vmap()))/reduce_sum | solution.py:97
  1179.9 34.8 %psum.7 = f32[3,33]{0,1:T(8,128)} all-reduce(f32[3,33]{0,1:T(8,128)} %pad_add_fusion.7), channel_id=1, replica_groups=mesh['dp'=8,'head'=4] {'dp'}, use_global_device_ids=true, to_apply=%region_64.65 | all-reduce | flops 99 | bytes 792 | tf_op jit(solution)/shard_map/psum | solution.py:198
  1218.9 37.9 %all-reduce.70 = bf16[9216]{0:T(1024)(128)(2,1)} all-reduce(bf16[9216]{0:T(1024)(128)(2,1)} %dynamic-update-slice), channel_id=1, replica_groups=mesh['dp'=8,'head'=4] {'dp','head'}, use_global_device_ids=true, to_apply=%add.70 | all-reduce | flops 9216 | bytes 36864
  1259.4 8.0 add_add_fusion.4
  1275.7 8.1 reshape.1886
  1283.8 12.1 all-gather.9.cloned.1.call-done
  1295.9 8.7 reshape.1890
  1304.7 56.0 %all-gather.11.cloned.1.call-done = bf16[2359296]{0:T(1024)(128)(2,1)} async-done(((bf16[73728]{0:T(1024)(128)(2,1)}), bf16[2359296]{0:T(1024)(128)(2,1)}) %all-gather.11.cloned.1.call-update) | async-done | bytes 4718608 | tf_op jit(solution)/shard_map/all_gather | solution.py:223
  1360.6 10.0 reshape.1892
  (508 shorter events, 182.3 us)
Async XLA Ops:
  32.2 77.0 %all-to-all-start = ((bf16[1024,3,768]{0,1,2:T(4,128)(2,1)}), bf16[1024,3,768]{0,1,2:T(4,128)(2,1)}, u32[]{:S(2)}, u32[]{:S(2)}) async-start(bf16[1024,3,768]{0,1,2:T(4,128)(2,1)} %copy.377), calls=%async_computation | async-start | bytes 12582912 | tf_op jit(solution)/shard_map/all_to_all | solution.py:147
  42.4 88.9 %copy-start.102 = (s32[64]{0:T(128)}, s32[64]{0:T(128)S(1)}, u32[]{:S(2)}) copy-start(s32[64]{0:T(128)S(1)} %get-tuple-element.242) | copy-start | bytes 772
  42.4 88.9 %copy-start.104 = (s32[64]{0:T(128)}, s32[64]{0:T(128)S(1)}, u32[]{:S(2)}) copy-start(s32[64]{0:T(128)S(1)} %get-tuple-element.243) | copy-start | bytes 772
  42.8 88.5 %copy-start.149 = (f32[64]{0:T(128)}, f32[64]{0:T(128)S(1)}, u32[]{:S(2)}) copy-start(f32[64]{0:T(128)S(1)} %convert_reduce_fusion.4) | copy-start | bytes 772
  135.2 16.6 %copy-start.72 = (f32[3,4096]{1,0:T(4,128)}, f32[3,4096]{1,0:T(4,128)S(1)}, u32[]{:S(2)}) copy-start(f32[3,4096]{1,0:T(4,128)S(1)} %get-tuple-element.248) | copy-start | bytes 147460
  135.2 17.7 %copy-start.7 = (f32[3,4096,64]{1,2,0:T(8,128)}, f32[3,4096,64]{1,2,0:T(8,128)S(1)}, u32[]{:S(2)}) copy-start(f32[3,4096,64]{1,2,0:T(8,128)S(1)} %get-tuple-element.249) | copy-start | bytes 9437188
  189.3 24.5 %all-to-all-start.1 = ((bf16[4,1024,192]{1,2,0:T(8,128)(2,1)}), bf16[4,1024,192]{1,2,0:T(8,128)(2,1)}, u32[]{:S(2)}, u32[]{:S(2)}) async-start(bf16[4,1024,192]{1,2,0:T(8,128)(2,1)} %copy.387), calls=%async_computation.1 | async-start | bytes 3145728 | tf_op jit(solution)/shard_map/all_to_all | solution.py:155
  217.8 52.5 %copy-start.11 = (f32[1024,768]{0,1:T(8,128)}, f32[1024,768]{0,1:T(8,128)S(1)}, u32[]{:S(2)}) copy-start(f32[1024,768]{0,1:T(8,128)S(1)} %get-tuple-element.251) | copy-start | bytes 9437188
  217.9 52.4 %copy-start.87 = (f32[1024]{0:T(1024)}, f32[1024]{0:T(1024)S(1)}, u32[]{:S(2)}) copy-start(f32[1024]{0:T(1024)S(1)} %broadcast_multiply_fusion.35) | copy-start | bytes 12292
  218.7 51.6 %copy-start.98 = (f32[1024]{0:T(1024)}, f32[1024]{0:T(1024)S(1)}, u32[]{:S(2)}) copy-start(f32[1024]{0:T(1024)S(1)} %fusion.163) | copy-start | bytes 12292
  245.6 15.1 %copy-start.43 = (bf16[1024,768]{0,1:T(8,128)(2,1)}, bf16[1024,768]{0,1:T(8,128)(2,1)S(1)}, u32[]{:S(2)}) copy-start(bf16[1024,768]{0,1:T(8,128)(2,1)S(1)} %get-tuple-element.191) | copy-start | bytes 4718596
  275.8 24.5 %all-to-all-start.2 = ((bf16[1024,4,192]{0,2,1:T(8,128)(2,1)}), bf16[1024,4,192]{0,2,1:T(8,128)(2,1)}, u32[]{:S(2)}, u32[]{:S(2)}) async-start(bf16[1024,4,192]{0,2,1:T(8,128)(2,1)} %bitcast.653), calls=%async_computation.2 | async-start | bytes 3145728 | tf_op jit(solution)/shard_map/all_to_all | solution.py:189
  336.7 15.0 %copy-start.108 = (f32[3]{0:T(128)S(1)}, f32[3]{0:T(128)}, u32[]{:S(2)}) copy-start(f32[3]{0:T(128)} %get-tuple-element.182) | copy-start | bytes 40
  336.7 15.0 %copy-start.109 = (f32[3]{0:T(128)S(1)}, f32[3]{0:T(128)}, u32[]{:S(2)}) copy-start(f32[3]{0:T(128)} %get-tuple-element.184) | copy-start | bytes 40
  336.7 15.0 %copy-start.125 = (f32[3]{0:T(128)S(1)}, f32[3]{0:T(128)}, u32[]{:S(2)}) copy-start(f32[3]{0:T(128)} %get-tuple-element.153) | copy-start | bytes 40
  336.7 15.0 %copy-start.126 = (f32[3]{0:T(128)S(1)}, f32[3]{0:T(128)}, u32[]{:S(2)}) copy-start(f32[3]{0:T(128)} %get-tuple-element.154) | copy-start | bytes 40
  336.7 15.0 %copy-start.127 = (f32[3]{0:T(128)S(1)}, f32[3]{0:T(128)}, u32[]{:S(2)}) copy-start(f32[3]{0:T(128)} %get-tuple-element.155) | copy-start | bytes 40
  336.7 15.0 %copy-start.128 = (f32[3]{0:T(128)S(1)}, f32[3]{0:T(128)}, u32[]{:S(2)}) copy-start(f32[3]{0:T(128)} %get-tuple-element.156) | copy-start | bytes 40
  336.7 15.0 %copy-start.129 = (f32[3]{0:T(128)S(1)}, f32[3]{0:T(128)}, u32[]{:S(2)}) copy-start(f32[3]{0:T(128)} %get-tuple-element.157) | copy-start | bytes 40
  336.7 15.0 %copy-start.130 = (f32[3]{0:T(128)S(1)}, f32[3]{0:T(128)}, u32[]{:S(2)}) copy-start(f32[3]{0:T(128)} %get-tuple-element.158) | copy-start | bytes 40
  336.7 15.0 %copy-start.131 = (f32[3]{0:T(128)S(1)}, f32[3]{0:T(128)}, u32[]{:S(2)}) copy-start(f32[3]{0:T(128)} %get-tuple-element.159) | copy-start | bytes 40
  336.8 15.0 %copy-start.132 = (f32[3]{0:T(128)S(1)}, f32[3]{0:T(128)}, u32[]{:S(2)}) copy-start(f32[3]{0:T(128)} %get-tuple-element.160) | copy-start | bytes 40
  336.8 15.0 %copy-start.133 = (f32[3]{0:T(128)S(1)}, f32[3]{0:T(128)}, u32[]{:S(2)}) copy-start(f32[3]{0:T(128)} %get-tuple-element.161) | copy-start | bytes 40
  336.8 15.0 %copy-start.134 = (f32[3]{0:T(128)S(1)}, f32[3]{0:T(128)}, u32[]{:S(2)}) copy-start(f32[3]{0:T(128)} %get-tuple-element.162) | copy-start | bytes 40
  336.8 15.0 %copy-start.135 = (f32[3]{0:T(128)S(1)}, f32[3]{0:T(128)}, u32[]{:S(2)}) copy-start(f32[3]{0:T(128)} %get-tuple-element.163) | copy-start | bytes 40
  452.3 15.8 %copy-start.26 = (f32[1,4096,1,3,64]{1,4,3,2,0:T(8,128)S(1)}, f32[1,4096,1,3,64]{1,4,3,2,0:T(8,128)}, u32[]{:S(2)}) copy-start(f32[1,4096,1,3,64]{1,4,3,2,0:T(8,128)} %fusion.7) | copy-start | bytes 9437188
  452.4 15.8 %copy-start.27 = (f32[1,4096,1,3,64]{1,4,3,2,0:T(8,128)S(1)}, f32[1,4096,1,3,64]{1,4,3,2,0:T(8,128)}, u32[]{:S(2)}) copy-start(f32[1,4096,1,3,64]{1,4,3,2,0:T(8,128)} %fusion.9) | copy-start | bytes 9437188
  483.5 98.8 %all-to-all-start.3 = ((bf16[4096,3,192]{2,1,0:T(4,128)(2,1)}), bf16[4096,3,192]{2,1,0:T(4,128)(2,1)}, u32[]{:S(2)}, u32[]{:S(2)}) async-start(bf16[4096,3,192]{2,1,0:T(4,128)(2,1)} %copy.437), calls=%async_computation.3 | async-start | bytes 16777216 | tf_op jit(solution)/shard_map/all_to_all | solution.py:191
  489.1 783.2 %all-gather.7.cloned.1.call-start = ((), (), s32[]{:S(2)}) async-start(), calls=%async_computation.5 | async-start | bytes 1216512 | tf_op jit(solution)/shard_map/all_gather | solution.py:217
  1116.8 158.8 %all-gather.5.cloned.1.call-start = ((), (), s32[]{:S(2)}) async-start(), calls=%async_computation.4 | async-start | bytes 3649536 | tf_op jit(solution)/shard_map/all_gather | solution.py:214
  1118.5 177.4 %all-gather.9.cloned.1.call-start = ((), (), s32[]{:S(2)}) async-start(), calls=%async_computation.6 | async-start | bytes 4866048 | tf_op jit(solution)/shard_map/all_gather | solution.py:220
  1120.1 240.5 %all-gather.11.cloned.1.call-start = ((), (), s32[]{:S(2)}) async-start(), calls=%async_computation.7 | async-start | bytes 4866048 | tf_op jit(solution)/shard_map/all_gather | solution.py:223
  1144.2 34.9 %copy-start.110 = (f32[3]{0:T(128)S(1)}, f32[3]{0:T(128)}, u32[]{:S(2)}) copy-start(f32[3]{0:T(128)} %get-tuple-element.129) | copy-start | bytes 40
  1144.2 34.9 %copy-start.111 = (f32[3]{0:T(128)S(1)}, f32[3]{0:T(128)}, u32[]{:S(2)}) copy-start(f32[3]{0:T(128)} %get-tuple-element.130) | copy-start | bytes 40
  1144.2 34.9 %copy-start.112 = (f32[3]{0:T(128)S(1)}, f32[3]{0:T(128)}, u32[]{:S(2)}) copy-start(f32[3]{0:T(128)} %get-tuple-element.131) | copy-start | bytes 40
  1144.2 34.9 %copy-start.113 = (f32[3]{0:T(128)S(1)}, f32[3]{0:T(128)}, u32[]{:S(2)}) copy-start(f32[3]{0:T(128)} %get-tuple-element.132) | copy-start | bytes 40
  1144.2 34.9 %copy-start.114 = (f32[3]{0:T(128)S(1)}, f32[3]{0:T(128)}, u32[]{:S(2)}) copy-start(f32[3]{0:T(128)} %get-tuple-element.133) | copy-start | bytes 40
  1144.2 34.9 %copy-start.115 = (f32[3]{0:T(128)S(1)}, f32[3]{0:T(128)}, u32[]{:S(2)}) copy-start(f32[3]{0:T(128)} %get-tuple-element.134) | copy-start | bytes 40
  1144.2 34.9 %copy-start.116 = (f32[3]{0:T(128)S(1)}, f32[3]{0:T(128)}, u32[]{:S(2)}) copy-start(f32[3]{0:T(128)} %get-tuple-element.135) | copy-start | bytes 40
  1144.2 34.9 %copy-start.117 = (f32[3]{0:T(128)S(1)}, f32[3]{0:T(128)}, u32[]{:S(2)}) copy-start(f32[3]{0:T(128)} %get-tuple-element.136) | copy-start | bytes 40
  1144.2 34.9 %copy-start.118 = (f32[3]{0:T(128)S(1)}, f32[3]{0:T(128)}, u32[]{:S(2)}) copy-start(f32[3]{0:T(128)} %get-tuple-element.137) | copy-start | bytes 40
  1144.2 34.9 %copy-start.119 = (f32[3]{0:T(128)S(1)}, f32[3]{0:T(128)}, u32[]{:S(2)}) copy-start(f32[3]{0:T(128)} %get-tuple-element.138) | copy-start | bytes 40
  1144.2 34.9 %copy-start.120 = (f32[3]{0:T(128)S(1)}, f32[3]{0:T(128)}, u32[]{:S(2)}) copy-start(f32[3]{0:T(128)} %get-tuple-element.139) | copy-start | bytes 40
  1144.3 34.9 %copy-start.121 = (f32[3]{0:T(128)S(1)}, f32[3]{0:T(128)}, u32[]{:S(2)}) copy-start(f32[3]{0:T(128)} %get-tuple-element.140) | copy-start | bytes 40
  1144.3 34.9 %copy-start.122 = (f32[3]{0:T(128)S(1)}, f32[3]{0:T(128)}, u32[]{:S(2)}) copy-start(f32[3]{0:T(128)} %get-tuple-element.141) | copy-start | bytes 40
  1144.3 34.9 %copy-start.123 = (f32[3]{0:T(128)S(1)}, f32[3]{0:T(128)}, u32[]{:S(2)}) copy-start(f32[3]{0:T(128)} %get-tuple-element.142) | copy-start | bytes 40
  1144.3 34.9 %copy-start.124 = (f32[3]{0:T(128)S(1)}, f32[3]{0:T(128)}, u32[]{:S(2)}) copy-start(f32[3]{0:T(128)} %get-tuple-element.143) | copy-start | bytes 40
  1144.3 34.9 %copy-start.139 = (f32[3]{0:T(128)S(1)}, f32[3]{0:T(128)}, u32[]{:S(2)}) copy-start(f32[3]{0:T(128)} %reduce_sum.603) | copy-start | bytes 40
  (119 other events, 588.2 us)
Sparse Core Ops, SparseCore 0:
  1117.0 51.8 all-gather.6
  1171.7 58.9 all-gather.4
  1233.6 62.2 all-gather.8
  1298.7 61.9 all-gather.10
where the time goes:
time: 1390 us; the launch traced here: 1380 us
  blocking collectives  531 us (38%)
  matrix products  219 us (16%)
  local copies, waits for them, and re-layouts  216 us (16%)
  waiting for transfers between devices  214 us (15%)
  other arithmetic  159 us (11%)
  starting transfers between devices  20.2 us (1%)
  between operations  17.5 us (1%)
    unnamed x2, blocking collectives  497 us
    all_to_all x1, waiting for transfers between devices, body(): lax.all_to_all(projected, 'head', split_axis=2, concat_axis=0, tiled=True)  66.4 us
    all_gather x1, waiting for transfers between devices, body(): lax.all_gather(part_down.astype(jnp.bfloat16), ('dp', 'head'), axis=0, ti...  56 us
    reduce_sum x4, other arithmetic, nystrom(): taps[None, :, tap_index, None] * padded[tap_index:tap_index + positions]  55.9 us
    all_to_all x1, waiting for transfers between devices, body(): lax.all_to_all(d_joined.astype(jnp.bfloat16), 'head', split_axis=0, conca...  50.4 us
    unnamed x339, local copies, waits for them, and re-layouts  43.3 us
    dot_general x3, matrix products, nystrom(): jnp.einsum('hnl,hld->nhd', first_kernel_matrix, mixed_value_rows, precisi...  42.6 us
    add_any x1, other arithmetic, nystrom(): padded[tap_index:tap_index + positions]  35.5 us
  transfers between devices with their start and end apart: 8, of which 6 were waited for; matrix products, arithmetic and copies ran while one was open for 12% of the time, Pallas kernels for 0%

commit v1 on v0

--- a/solution.py
+++ b/solution.py
@@ -188,8 +188,14 @@
     )
     d_heads = lax.all_to_all(d_context, "head", split_axis=1, concat_axis=0, tiled=True)
     d_joined, d_taps = attend_back(d_heads.astype(jnp.float32))
-    d_proj = lax.all_to_all(
-        d_joined.astype(jnp.bfloat16), "head", split_axis=0, concat_axis=2, tiled=True
+    d_proj = jnp.concatenate(
+        lax.all_to_all(
+            jnp.stack(jnp.split(d_joined.astype(jnp.bfloat16), lax.axis_size("head"), axis=0)),
+            "head",
+            0,
+            0,
+        ),
+        axis=2,
     ).reshape(tok_rows, 3 * width)
     g_qkv = jnp.einsum("td,tk->dk", tokens, d_proj, preferred_element_type=jnp.float32)
     proj_sums = jnp.sum(d_proj.astype(jnp.float32), axis=0)

time: 1390 us -> 1310 us (0.942)
  local copies, waits for them, and re-layouts: 216 us -> 179 us
  waiting for transfers between devices: 214 us -> 177 us
    all_to_all x1, waiting for transfers between devices: 50.4 us -> 11.1 us  [body(): lax.all_to_all(jnp.stack(jnp.split(d_joined.astype(jnp.bfloat16), lax.axi...]
    all_to_all x2 -> x1, local copies, waits for them, and re-layouts: 26.5 us -> 2.96 us  [body(): lax.all_to_all(jnp.stack(jnp.split(d_joined.astype(jnp.bfloat16), lax.axi...]
    unnamed x339 -> x343, local copies, waits for them, and re-layouts: 43.3 us -> 45.5 us
where the time goes in v1:
time: 1310 us; the launch traced here: 1300 us
  blocking collectives  532 us (41%)
  matrix products  215 us (16%)
  local copies, waits for them, and re-layouts  179 us (14%)
  waiting for transfers between devices  177 us (14%)
  other arithmetic  157 us (12%)
  starting transfers between devices  19.4 us (1%)
  between operations  17.8 us (1%)
    unnamed x2, blocking collectives  497 us
    all_to_all x1, waiting for transfers between devices, body(): lax.all_to_all(projected, 'head', split_axis=2, concat_axis=0, tiled=True)  66.4 us
    all_gather x1, waiting for transfers between devices, body(): lax.all_gather(part_down.astype(jnp.bfloat16), ('dp', 'head'), axis=0, ti...  56 us
    reduce_sum x4, other arithmetic, nystrom(): taps[None, :, tap_index, None] * padded[tap_index:tap_index + positions]  54.3 us
    unnamed x343, local copies, waits for them, and re-layouts  45.5 us
    dot_general x3, matrix products, nystrom(): jnp.einsum('hnl,hld->nhd', first_kernel_matrix, mixed_value_rows, precisi...  42.6 us
    add_any x1, other arithmetic, nystrom(): padded[tap_index:tap_index + positions]  35.8 us
    psum x1, blocking collectives, body(): g_taps = lax.psum(d_taps, 'dp')  34.8 us
  transfers between devices with their start and end apart: 8, of which 6 were waited for; matrix products, arithmetic and copies ran while one was open for 12% of the time, Pallas kernels for 0%

profile of v1, /device:TPU:0, one launch (start us, length us, event | category | flops | bytes accessed | tf_op | source)
XLA Modules:
  0.0 1297.0 jit_solution(4846254014554927203)
XLA Ops:
  9.2 7.3 add_convert_fusion.2
  16.5 6.6 copy.237
  23.1 9.1 copy.238
  32.2 5.6 all-to-all-start
  42.8 66.4 %all-to-all-done = bf16[1024,3,768]{0,1,2:T(4,128)(2,1)} async-done(((bf16[1024,3,768]{0,1,2:T(4,128)(2,1)}), bf16[1024,3,768]{0,1,2:T(4,128)(2,1)}, u32[]{:S(2)}, u32[]{:S(2)}) %all-to-all-start) | async-done | bytes 4718624 | tf_op jit(solution)/shard_map/all_to_all | solution.py:147
  109.1 4.7 copy.239
  113.8 5.8 copy.240
  119.6 9.1 reshape.1847
  152.8 29.3 %fusion.10 = bf16[1,4096,3,64]{1,3,2,0:T(8,128)(2,1)} fusion(f32[3,64,64]{2,1,0:T(8,128)S(1)} %copy-done.76, f32[3]{0:T(128)} %get-tuple-element.151, f32[3]{0:T(128)} %get-tuple-element.152, f32[3]{0:T(128)} %get-tuple-element.121, f32[3]{0:T(128)} %get-tuple-element.122, f32[3]{0:T(128)} %get-tuple-element.123, f32[3]{0:T(128)} %get-tuple-element.124, ...), kind=kOutput, calls=%fused_computation.26 | convolution fusion | flops 660602880 | bytes 9601420 | tf_op jit(solution)/shard_map/jvp(vmap(hnl,hld->nhd))/dot_general | solution.py:89
  189.1 4.3 all-to-all-start.1
  200.6 13.1 %all-to-all-done.1 = bf16[4,1024,192]{1,2,0:T(8,128)(2,1)} async-done(((bf16[4,1024,192]{1,2,0:T(8,128)(2,1)}), bf16[4,1024,192]{1,2,0:T(8,128)(2,1)}, u32[]{:S(2)}, u32[]{:S(2)}) %all-to-all-start.1) | async-done | bytes 1572896 | tf_op jit(solution)/shard_map/all_to_all | solution.py:155
  218.5 11.3 multiply_convert_fusion
  229.9 7.8 fusion.206
  245.5 15.1 %convert_reduce_fusion = (f32[3072]{0:T(1024)}, bf16[1024,3072]{1,0:T(8,128)(2,1)}) fusion(bf16[1024,768]{0,1:T(8,128)(2,1)S(1)} %get-tuple-element.159, bf16[3072,768]{1,0:T(8,128)(2,1)S(1)} %bitcast.692, f32[1024,3072]{1,0:T(8,128)} %get-tuple-element.225, f32[3072]{0:T(1024)S(1)} %copy-done.148), kind=kOutput, calls=%fused_computation | convolution fusion | flops 4882166784 | bytes 25190400 | tf_op jit(solution)/shard_map/td,kd->tk/dot_general | solution.py:174
  260.6 9.5 multiply_reduce_fusion.33
  275.6 4.4 all-to-all-start.2
  283.9 16.2 %all-to-all-done.2 = bf16[1024,4,192]{0,2,1:T(8,128)(2,1)} async-done(((bf16[1024,4,192]{0,2,1:T(8,128)(2,1)}), bf16[1024,4,192]{0,2,1:T(8,128)(2,1)}, u32[]{:S(2)}, u32[]{:S(2)}) %all-to-all-start.2) | async-done | bytes 1572896 | tf_op jit(solution)/shard_map/all_to_all | solution.py:189
  305.7 5.4 reshape.1891
  311.2 6.5 fusion.13
  336.7 14.8 %multiply_reduce_fusion.30 = (f32[3]{0:T(128)}, f32[3]{0:T(128)}, f32[3]{0:T(128)}, f32[3]{0:T(128)}, f32[3]{0:T(128)}, /*index=5*/f32[3]{0:T(128)}, f32[3]{0:T(...) fusion(f32[1,4096,3,64]{1,3,2,0:T(8,128)S(1)} %copy-done.6, ...), kind=kLoop, calls=%fused_computation.78 | loop fusion | flops 25952208 | bytes 12599500 | tf_op jit(solution)/shard_map/transpose(jvp(vmap()))/reduce_sum | solution.py:97
  351.6 14.3 %broadcast_multiply_fusion.1 = (f32[1,4096,3,64]{1,3,2,0:T(8,128)}, f32[1,4096,3,64]{1,3,2,0:T(8,128)}, f32[1,4096,3,64]{1,3,2,0:T(8,128)}, f32[1,4096,3,64]{1,3...) fusion(f32[3]{0:T(128)S(1)} %copy-done.111, ...), kind=kLoop, calls=%fused_computation.118 | loop fusion | flops 11796480 | bytes 47202472 | tf_op jit(solution)/shard_map/transpose(jvp(vmap()))/mul | solution.py:97
  365.9 18.9 %broadcast_multiply_fusion = (f32[1,4096,3,64]{1,3,2,0:T(8,128)}, f32[1,4096,3,64]{1,3,2,0:T(8,128)}, f32[1,4096,3,64]{1,3,2,0:T(8,128)}, f32[1,4096,3,64]{1,3,2...) fusion(f32[3]{0:T(128)} %get-tuple-element.151, ...), kind=kLoop, calls=%fused_computation.117 | loop fusion | flops 14155776 | bytes 56639692 | tf_op jit(solution)/shard_map/transpose(jvp(vmap()))/mul | solution.py:97
  384.9 6.8 multiply_reduce_fusion.34
  403.6 5.7 fusion.7
  410.8 5.6 fusion.9
  416.4 35.8 %pad_add_fusion = f32[1,4128,3,64]{1,3,2,0:T(8,128)} fusion(f32[1,4096,3,64]{1,3,2,0:T(8,128)} %get-tuple-element.174, f32[1,4096,3,64]{1,3,2,0:T(8,128)} %get-tuple-element.175, f32[1,4096,3,64]{1,3,2,0:T(8,128)} %get-tuple-element.176, f32[1,4096,3,64]{1,3,2,0:T(8,128)} %get-tuple-element.177, f32[1,4096,3,64]{1,3,2,0:T(8,128)} %get-tuple-element.178, ...), kind=kLoop, calls=%fused_computation.31 | loop fusion | flops 20606976 | bytes 88104960 | tf_op jit(solution)/shard_map/transpose(jvp(vmap()))/add_any | solution.py:97
  452.3 15.8 %fusion.5 = f32[1,4096,1,3,64]{1,4,3,2,0:T(8,128)S(1)} fusion(f32[3,64,64]{2,1,0:T(8,128)} %fusion.208, f32[1,4096,3,64]{1,3,2,0:T(8,128)} %get-tuple-element.169, f32[1,4096,3,64]{1,3,2,0:T(8,128)} %get-tuple-element.168, f32[1,4096,3,64]{1,3,2,0:T(8,128)} %get-tuple-element.200, f32[1,4096,3,64]{1,3,2,0:T(8,128)} %get-tuple-element.171, ...), kind=kOutput, calls=%fused_computation.21 | convolution fusion | flops 611844096 | bytes 28378624 | tf_op jit(solution)/shard_map/transpose(jvp(vmap(qbl,lqs->qbs)))/dot_general | solution.py:83
  471.8 4.9 all-to-all-start.3
  476.8 8.5 convolution_bitcast_fusion.7
  485.4 5.9 copy.362
  498.8 9.9 fusion.217
  508.7 10.8 reshape.1888
  519.5 11.1 all-to-all-done.3
  553.8 5.8 convolution_bitcast_fusion
  559.6 8.0 copy.300
  567.6 7.9 reshape.1879
  575.5 458.9 %all-reduce.78 = (bf16[9216]{0:T(1024)(128)(2,1)}, bf16[1769472]{0:T(1024)(128)(2,1)}, bf16[589824]{0:T(1024)(128)(2,1)}, bf16[2359296]{0:T(1024)(128)(2,1)}, bf16[2359296]{0:T(1024)(128)(2,1)}) all-reduce(f32[9216]{0:T(1024)} %constant_dynamic-update-slice_fusion, ...), channel_id=3, replica_groups=mesh['dp'=8,'head'=4] {'dp','head'}, use_global_device_ids=true, to_apply=%region_29.30.clone | all-reduce | flops 7087104 | bytes 42522624
  1045.4 5.2 squeeze.8
  1055.1 4.9 fusion.16
  1062.8 33.2 %multiply_reduce_fusion.31 = (f32[3]{0:T(128)S(1)}, f32[3]{0:T(128)S(1)}, f32[3]{0:T(128)S(1)}, f32[3]{0:T(128)S(1)}, f32[3]{0:T(128)S(1)}, /*index=5*/f32[3]{0:...) fusion(f32[1,4096,3,64]{1,3,2,0:T(8,128)} %copy-done.5, ...), kind=kLoop, calls=%fused_computation.79 | loop fusion | flops 27525064 | bytes 6308044 | tf_op jit(solution)/shard_map/transpose(jvp(vmap()))/reduce_sum | solution.py:97
  1096.9 34.8 %psum.7 = f32[3,33]{0,1:T(8,128)} all-reduce(f32[3,33]{0,1:T(8,128)} %pad_add_fusion.7), channel_id=1, replica_groups=mesh['dp'=8,'head'=4] {'dp'}, use_global_device_ids=true, to_apply=%region_64.65 | all-reduce | flops 99 | bytes 792 | tf_op jit(solution)/shard_map/psum | solution.py:204
  1135.9 37.9 %all-reduce.70 = bf16[9216]{0:T(1024)(128)(2,1)} all-reduce(bf16[9216]{0:T(1024)(128)(2,1)} %dynamic-update-slice), channel_id=1, replica_groups=mesh['dp'=8,'head'=4] {'dp','head'}, use_global_device_ids=true, to_apply=%add.70 | all-reduce | flops 9216 | bytes 36864
  1176.4 8.1 add_add_fusion.4
  1192.8 8.0 reshape.1893
  1200.8 14.6 %all-gather.9.cloned.1.call-done = bf16[2359296]{0:T(1024)(128)(2,1)} async-done(((bf16[73728]{0:T(1024)(128)(2,1)}), bf16[2359296]{0:T(1024)(128)(2,1)}) %all-gather.9.cloned.1.call-update) | async-done | bytes 4718608 | tf_op jit(solution)/shard_map/all_gather | solution.py:226
  1215.4 8.7 reshape.1897
  1224.1 56.0 %all-gather.11.cloned.1.call-done = bf16[2359296]{0:T(1024)(128)(2,1)} async-done(((bf16[73728]{0:T(1024)(128)(2,1)}), bf16[2359296]{0:T(1024)(128)(2,1)}) %all-gather.11.cloned.1.call-update) | async-done | bytes 4718608 | tf_op jit(solution)/shard_map/all_gather | solution.py:229
  1280.1 10.0 reshape.1899
  (510 shorter events, 170.8 us)
Async XLA Ops:
  32.2 77.0 %all-to-all-start = ((bf16[1024,3,768]{0,1,2:T(4,128)(2,1)}), bf16[1024,3,768]{0,1,2:T(4,128)(2,1)}, u32[]{:S(2)}, u32[]{:S(2)}) async-start(bf16[1024,3,768]{0,1,2:T(4,128)(2,1)} %copy.238), calls=%async_computation | async-start | bytes 12582912 | tf_op jit(solution)/shard_map/all_to_all | solution.py:147
  42.4 88.8 %copy-start.104 = (s32[64]{0:T(128)}, s32[64]{0:T(128)S(1)}, u32[]{:S(2)}) copy-start(s32[64]{0:T(128)S(1)} %get-tuple-element.214) | copy-start | bytes 772
  42.4 88.8 %copy-start.106 = (s32[64]{0:T(128)}, s32[64]{0:T(128)S(1)}, u32[]{:S(2)}) copy-start(s32[64]{0:T(128)S(1)} %get-tuple-element.215) | copy-start | bytes 772
  42.8 88.4 %copy-start.151 = (f32[64]{0:T(128)}, f32[64]{0:T(128)S(1)}, u32[]{:S(2)}) copy-start(f32[64]{0:T(128)S(1)} %convert_reduce_fusion.4) | copy-start | bytes 772
  135.0 16.6 %copy-start.74 = (f32[3,4096]{1,0:T(4,128)}, f32[3,4096]{1,0:T(4,128)S(1)}, u32[]{:S(2)}) copy-start(f32[3,4096]{1,0:T(4,128)S(1)} %get-tuple-element.220) | copy-start | bytes 147460
  135.0 17.7 %copy-start.7 = (f32[3,4096,64]{1,2,0:T(8,128)}, f32[3,4096,64]{1,2,0:T(8,128)S(1)}, u32[]{:S(2)}) copy-start(f32[3,4096,64]{1,2,0:T(8,128)S(1)} %get-tuple-element.221) | copy-start | bytes 9437188
  189.1 24.5 %all-to-all-start.1 = ((bf16[4,1024,192]{1,2,0:T(8,128)(2,1)}), bf16[4,1024,192]{1,2,0:T(8,128)(2,1)}, u32[]{:S(2)}, u32[]{:S(2)}) async-start(bf16[4,1024,192]{1,2,0:T(8,128)(2,1)} %copy.248), calls=%async_computation.1 | async-start | bytes 3145728 | tf_op jit(solution)/shard_map/all_to_all | solution.py:155
  217.7 52.4 %copy-start.11 = (f32[1024,768]{0,1:T(8,128)}, f32[1024,768]{0,1:T(8,128)S(1)}, u32[]{:S(2)}) copy-start(f32[1024,768]{0,1:T(8,128)S(1)} %get-tuple-element.223) | copy-start | bytes 9437188
  217.7 52.4 %copy-start.89 = (f32[1024]{0:T(1024)}, f32[1024]{0:T(1024)S(1)}, u32[]{:S(2)}) copy-start(f32[1024]{0:T(1024)S(1)} %broadcast_multiply_fusion.35) | copy-start | bytes 12292
  218.5 51.6 %copy-start.100 = (f32[1024]{0:T(1024)}, f32[1024]{0:T(1024)S(1)}, u32[]{:S(2)}) copy-start(f32[1024]{0:T(1024)S(1)} %fusion.163) | copy-start | bytes 12292
  245.5 15.1 %copy-start.45 = (bf16[1024,768]{0,1:T(8,128)(2,1)}, bf16[1024,768]{0,1:T(8,128)(2,1)S(1)}, u32[]{:S(2)}) copy-start(bf16[1024,768]{0,1:T(8,128)(2,1)S(1)} %get-tuple-element.159) | copy-start | bytes 4718596
  275.6 24.5 %all-to-all-start.2 = ((bf16[1024,4,192]{0,2,1:T(8,128)(2,1)}), bf16[1024,4,192]{0,2,1:T(8,128)(2,1)}, u32[]{:S(2)}, u32[]{:S(2)}) async-start(bf16[1024,4,192]{0,2,1:T(8,128)(2,1)} %bitcast.657), calls=%async_computation.2 | async-start | bytes 3145728 | tf_op jit(solution)/shard_map/all_to_all | solution.py:189
  336.5 15.0 %copy-start.110 = (f32[3]{0:T(128)S(1)}, f32[3]{0:T(128)}, u32[]{:S(2)}) copy-start(f32[3]{0:T(128)} %get-tuple-element.150) | copy-start | bytes 40
  336.6 15.0 %copy-start.111 = (f32[3]{0:T(128)S(1)}, f32[3]{0:T(128)}, u32[]{:S(2)}) copy-start(f32[3]{0:T(128)} %get-tuple-element.152) | copy-start | bytes 40
  336.6 15.0 %copy-start.127 = (f32[3]{0:T(128)S(1)}, f32[3]{0:T(128)}, u32[]{:S(2)}) copy-start(f32[3]{0:T(128)} %get-tuple-element.121) | copy-start | bytes 40
  336.6 15.0 %copy-start.128 = (f32[3]{0:T(128)S(1)}, f32[3]{0:T(128)}, u32[]{:S(2)}) copy-start(f32[3]{0:T(128)} %get-tuple-element.122) | copy-start | bytes 40
  336.6 14.9 %copy-start.129 = (f32[3]{0:T(128)S(1)}, f32[3]{0:T(128)}, u32[]{:S(2)}) copy-start(f32[3]{0:T(128)} %get-tuple-element.123) | copy-start | bytes 40
  336.6 14.9 %copy-start.130 = (f32[3]{0:T(128)S(1)}, f32[3]{0:T(128)}, u32[]{:S(2)}) copy-start(f32[3]{0:T(128)} %get-tuple-element.124) | copy-start | bytes 40
  336.6 14.9 %copy-start.131 = (f32[3]{0:T(128)S(1)}, f32[3]{0:T(128)}, u32[]{:S(2)}) copy-start(f32[3]{0:T(128)} %get-tuple-element.125) | copy-start | bytes 40
  336.6 14.9 %copy-start.132 = (f32[3]{0:T(128)S(1)}, f32[3]{0:T(128)}, u32[]{:S(2)}) copy-start(f32[3]{0:T(128)} %get-tuple-element.126) | copy-start | bytes 40
  336.6 14.9 %copy-start.133 = (f32[3]{0:T(128)S(1)}, f32[3]{0:T(128)}, u32[]{:S(2)}) copy-start(f32[3]{0:T(128)} %get-tuple-element.127) | copy-start | bytes 40
  336.6 14.9 %copy-start.134 = (f32[3]{0:T(128)S(1)}, f32[3]{0:T(128)}, u32[]{:S(2)}) copy-start(f32[3]{0:T(128)} %get-tuple-element.128) | copy-start | bytes 40
  336.6 14.9 %copy-start.135 = (f32[3]{0:T(128)S(1)}, f32[3]{0:T(128)}, u32[]{:S(2)}) copy-start(f32[3]{0:T(128)} %get-tuple-element.129) | copy-start | bytes 40
  336.7 14.9 %copy-start.136 = (f32[3]{0:T(128)S(1)}, f32[3]{0:T(128)}, u32[]{:S(2)}) copy-start(f32[3]{0:T(128)} %get-tuple-element.130) | copy-start | bytes 40
  336.7 14.9 %copy-start.137 = (f32[3]{0:T(128)S(1)}, f32[3]{0:T(128)}, u32[]{:S(2)}) copy-start(f32[3]{0:T(128)} %get-tuple-element.131) | copy-start | bytes 40
  452.2 15.8 %copy-start.27 = (f32[1,4096,1,3,64]{1,4,3,2,0:T(8,128)S(1)}, f32[1,4096,1,3,64]{1,4,3,2,0:T(8,128)}, u32[]{:S(2)}) copy-start(f32[1,4096,1,3,64]{1,4,3,2,0:T(8,128)} %fusion.7) | copy-start | bytes 9437188
  452.2 15.8 %copy-start.28 = (f32[1,4096,1,3,64]{1,4,3,2,0:T(8,128)S(1)}, f32[1,4096,1,3,64]{1,4,3,2,0:T(8,128)}, u32[]{:S(2)}) copy-start(f32[1,4096,1,3,64]{1,4,3,2,0:T(8,128)} %fusion.9) | copy-start | bytes 9437188
  471.8 58.8 %all-to-all-start.3 = ((bf16[4,1024,3,192]{1,3,2,0:T(8,128)(2,1)}), bf16[4,1024,3,192]{1,3,2,0:T(8,128)(2,1)}, u32[]{:S(2)}, u32[]{:S(2)}) async-start(bf16[4,1024,3,192]{1,3,2,0:T(8,128)(2,1)} %pad_maximum_fusion), calls=%async_computation.3 | async-start | bytes 9437184 | tf_op jit(solution)/shard_map/all_to_all | solution.py:192
  476.7 712.7 %all-gather.7.cloned.1.call-start = ((), (), s32[]{:S(2)}) async-start(), calls=%async_computation.5 | async-start | bytes 1216512 | tf_op jit(solution)/shard_map/all_gather | solution.py:223
  1035.8 157.0 %all-gather.5.cloned.1.call-start = ((), (), s32[]{:S(2)}) async-start(), calls=%async_computation.4 | async-start | bytes 3649536 | tf_op jit(solution)/shard_map/all_gather | solution.py:220
  1037.4 178.0 %all-gather.9.cloned.1.call-start = ((), (), s32[]{:S(2)}) async-start(), calls=%async_computation.6 | async-start | bytes 4866048 | tf_op jit(solution)/shard_map/all_gather | solution.py:226
  1039.1 241.0 %all-gather.11.cloned.1.call-start = ((), (), s32[]{:S(2)}) async-start(), calls=%async_computation.7 | async-start | bytes 4866048 | tf_op jit(solution)/shard_map/all_gather | solution.py:229
  1062.7 33.4 %copy-start.112 = (f32[3]{0:T(128)S(1)}, f32[3]{0:T(128)}, u32[]{:S(2)}) copy-start(f32[3]{0:T(128)} %get-tuple-element.97) | copy-start | bytes 40
  1062.7 33.4 %copy-start.113 = (f32[3]{0:T(128)S(1)}, f32[3]{0:T(128)}, u32[]{:S(2)}) copy-start(f32[3]{0:T(128)} %get-tuple-element.98) | copy-start | bytes 40
  1062.7 33.4 %copy-start.114 = (f32[3]{0:T(128)S(1)}, f32[3]{0:T(128)}, u32[]{:S(2)}) copy-start(f32[3]{0:T(128)} %get-tuple-element.99) | copy-start | bytes 40
  1062.7 33.4 %copy-start.115 = (f32[3]{0:T(128)S(1)}, f32[3]{0:T(128)}, u32[]{:S(2)}) copy-start(f32[3]{0:T(128)} %get-tuple-element.100) | copy-start | bytes 40
  1062.7 33.4 %copy-start.116 = (f32[3]{0:T(128)S(1)}, f32[3]{0:T(128)}, u32[]{:S(2)}) copy-start(f32[3]{0:T(128)} %get-tuple-element.101) | copy-start | bytes 40
  1062.7 33.4 %copy-start.117 = (f32[3]{0:T(128)S(1)}, f32[3]{0:T(128)}, u32[]{:S(2)}) copy-start(f32[3]{0:T(128)} %get-tuple-element.102) | copy-start | bytes 40
  1062.7 33.4 %copy-start.118 = (f32[3]{0:T(128)S(1)}, f32[3]{0:T(128)}, u32[]{:S(2)}) copy-start(f32[3]{0:T(128)} %get-tuple-element.103) | copy-start | bytes 40
  1062.7 33.4 %copy-start.119 = (f32[3]{0:T(128)S(1)}, f32[3]{0:T(128)}, u32[]{:S(2)}) copy-start(f32[3]{0:T(128)} %get-tuple-element.104) | copy-start | bytes 40
  1062.7 33.4 %copy-start.120 = (f32[3]{0:T(128)S(1)}, f32[3]{0:T(128)}, u32[]{:S(2)}) copy-start(f32[3]{0:T(128)} %get-tuple-element.105) | copy-start | bytes 40
  1062.8 33.4 %copy-start.121 = (f32[3]{0:T(128)S(1)}, f32[3]{0:T(128)}, u32[]{:S(2)}) copy-start(f32[3]{0:T(128)} %get-tuple-element.106) | copy-start | bytes 40
  1062.8 33.4 %copy-start.122 = (f32[3]{0:T(128)S(1)}, f32[3]{0:T(128)}, u32[]{:S(2)}) copy-start(f32[3]{0:T(128)} %get-tuple-element.107) | copy-start | bytes 40
  1062.8 33.4 %copy-start.123 = (f32[3]{0:T(128)S(1)}, f32[3]{0:T(128)}, u32[]{:S(2)}) copy-start(f32[3]{0:T(128)} %get-tuple-element.108) | copy-start | bytes 40
  1062.8 33.4 %copy-start.124 = (f32[3]{0:T(128)S(1)}, f32[3]{0:T(128)}, u32[]{:S(2)}) copy-start(f32[3]{0:T(128)} %get-tuple-element.109) | copy-start | bytes 40
  1062.8 33.4 %copy-start.125 = (f32[3]{0:T(128)S(1)}, f32[3]{0:T(128)}, u32[]{:S(2)}) copy-start(f32[3]{0:T(128)} %get-tuple-element.110) | copy-start | bytes 40
  1062.8 33.4 %copy-start.126 = (f32[3]{0:T(128)S(1)}, f32[3]{0:T(128)}, u32[]{:S(2)}) copy-start(f32[3]{0:T(128)} %get-tuple-element.111) | copy-start | bytes 40
  1062.8 33.4 %copy-start.141 = (f32[3]{0:T(128)S(1)}, f32[3]{0:T(128)}, u32[]{:S(2)}) copy-start(f32[3]{0:T(128)} %reduce_sum.603) | copy-start | bytes 40
  (121 other events, 595.4 us)
Sparse Core Ops, SparseCore 0:
  1035.9 51.8 all-gather.6
  1090.6 59.2 all-gather.4
  1152.8 62.5 all-gather.8
  1218.1 61.9 all-gather.10
